TPU v7x, 32 devices: a whole 2x2x4 slice. The times are simulated.
32 devices in a mesh: gx: 2 (over x), yz: 16 (over z, y, core).
Axes of the slice: x: 2, y: 2, z: 4, core: 2. Of those that a mesh axis runs over, the one named last changes fastest.
Arguments:
- tensor: float32 [4, 512, 32, 32], P(None, 'gx', 'yz'), may hold values from -40 to 40
- start_basis: float32 [96, 512], replicated, may hold values from -6 to 6
Outputs:
- core_tensor: float32 [32, 32, 384], P(('gx', 'yz'))
- factor: float32 [96, 512], replicated
All inputs are finite; a program needn't handle non-finite values.
Results may differ from a plain program's by a relative error of at most 0.00012.
Values sent between devices are 32-bit elements; how exact they have to be, the bound alone decides.
A program may use at most 64 MiB of HBM per device.

v0:
```python
import jax
import jax.numpy as jnp
from jax import lax
from jax.sharding import PartitionSpec as P


def orthonormal(image_rows):
    small_gram = jnp.dot(image_rows, image_rows.T, precision=lax.Precision.HIGHEST)
    lower_factor = jnp.linalg.cholesky(small_gram)
    return lax.linalg.triangular_solve(lower_factor, image_rows, left_side=True, lower=True)


def fibre_gram(left_part, right_part):
    return lax.dot_general(
        left_part, right_part, (((0, 2, 3), (0, 2, 3)), ((), ())), precision=lax.Precision.HIGHEST
    )


def local(tensor, start_basis):
    regrouped = lax.all_to_all(tensor, "gx", split_axis=2, concat_axis=1, tiled=True)
    species, width_x, lines, cells_z = regrouped.shape
    cell_count = species * lines * lax.axis_size("gx") * lax.axis_size("yz") * cells_z
    gram_matrix = lax.psum(fibre_gram(regrouped, regrouped), ("gx", "yz")) / cell_count
    basis = start_basis
    for repeat in range(2):
        basis = orthonormal(jnp.dot(basis, gram_matrix, precision=lax.Precision.HIGHEST))
    core_local = jnp.einsum("kx,sxyz->zysk", basis, regrouped, precision=lax.Precision.HIGHEST)
    core_local = core_local.reshape(cells_z, lines, species * basis.shape[0])
    core_tensor = lax.all_to_all(
        lax.all_to_all(core_local, "gx", split_axis=0, concat_axis=1, tiled=True),
        "yz",
        split_axis=0,
        concat_axis=1,
        tiled=True,
    )
    return (core_tensor, basis)


def solution(mesh):
    placed = (P(None, "gx", "yz", None), P())
    return jax.shard_map(
        local,
        mesh=mesh,
        in_specs=placed,
        out_specs=(P(("gx", "yz"), None, None), P()),
        check_vma=False,
    )
```

profile of v0, /device:TPU:0, one launch (start us, length us, event | category | flops | bytes accessed | tf_op | source)
XLA Modules:
  0.0 216.7 jit_solution(6574498621706970048)
XLA Ops:
  7.2 1.0 copy.16
  8.2 9.2 %all_to_all.45 = f32[4,256,2,32]{1,3,0,2:T(8,128)S(1)} all-to-all(f32[4,256,2,32]{1,3,0,2:T(8,128)S(1)} %copy.16), channel_id=1, replica_groups=mesh['gx'=2,'yz'=16] {'gx'}, dimensions={2} | all-to-all | bytes 524288 | tf_op jit(solution)/shard_map/all_to_all | solution.py:20
  17.7 0.2 reshape.30
  17.9 2.1 convolution_bitcast_fusion
  20.0 131.3 %all-reduce.2.cloned.1.call-done = f32[512,512]{1,0:T(8,128)} async-done(((f32[512,512]{1,0:T(8,128)}), f32[512,512]{1,0:T(8,128)}) %all-reduce.2.cloned.1.call-update) | async-done | bytes 1048592 | tf_op jit(solution)/shard_map/psum | solution.py:23
  151.3 2.1 fusion.2
  153.4 0.3 fusion.19
  153.8 8.8 %cholesky.44 = f32[96,96]{1,0:T(8,128)S(1)} custom-call(f32[96,96]{1,0:T(8,128)S(1)} %fusion.14), custom_call_target="Cholesky" | custom-call | tf_op jit(solution)/shard_map/jit(cholesky)/cholesky | solution.py:9
  162.6 0.6 compare_reduce_fusion.1
  163.3 0.7 fusion.8
  163.9 7.4 %custom-call.6 = f32[1,96,96]{1,2,0:T(8,128)S(1)} custom-call(f32[1,96,96]{2,1,0:T(8,128)S(1)} %fusion.8), custom_call_target="InvertDiagBlocksLowerTriangular" | custom-call | tf_op jit(solution)/shard_map/triangular_solve/custom-call.0 | solution.py:10
  171.3 0.4 fusion.6
  171.7 0.8 fusion
  172.5 0.3 fusion.20
  172.9 8.8 %cholesky.55 = f32[96,96]{1,0:T(8,128)S(1)} custom-call(f32[96,96]{1,0:T(8,128)S(1)} %fusion.12), custom_call_target="Cholesky" | custom-call | tf_op jit(solution)/shard_map/jit(cholesky)/cholesky | solution.py:9
  181.7 0.6 compare_reduce_fusion
  182.3 0.7 fusion.9
  183.0 7.4 %custom-call.7 = f32[1,96,96]{1,2,0:T(8,128)S(1)} custom-call(f32[1,96,96]{2,1,0:T(8,128)S(1)} %fusion.9), custom_call_target="InvertDiagBlocksLowerTriangular" | custom-call | tf_op jit(solution)/shard_map/triangular_solve/custom-call.0 | solution.py:10
  190.4 0.4 fusion.10
  190.8 0.4 fusion.21
  191.1 0.3 copy-done.2
  191.6 6.6 %all_to_all.46 = f32[32,1,384]{2,1,0:T(1,128)S(1)} all-to-all(f32[32,1,384]{2,1,0:T(1,128)S(1)} %reshape.41), channel_id=1, replica_groups=mesh['gx'=2,'yz'=16] {'gx'}, dimensions={0} | all-to-all | bytes 98304 | tf_op jit(solution)/shard_map/all_to_all | solution.py:30
  198.2 10.9 %all_to_all.47 = f32[16,2,384]{2,1,0:T(2,128)S(1)} all-to-all(f32[16,2,384]{2,1,0:T(2,128)S(1)} %copy.22), channel_id=1, replica_groups=mesh['gx'=2,'yz'=16] {'yz'}, dimensions={0} | all-to-all | bytes 98304 | tf_op jit(solution)/shard_map/all_to_all | solution.py:29
  209.2 0.7 all_to_all.41
  (18 shorter events, 0.7 us)
Async XLA Ops:
  7.2 144.1 %copy-start = (f32[96,512]{1,0:T(8,128)S(1)}, f32[96,512]{1,0:T(8,128)}, u32[]{:S(2)}) copy-start(f32[96,512]{1,0:T(8,128)} %param.6) | copy-start | bytes 589828
  7.2 144.1 %all-reduce.2.cloned.1.call-start = ((), (), s32[]{:S(2)}) async-start(), calls=%async_computation.3 | async-start | bytes 2097152 | tf_op jit(solution)/shard_map/psum | solution.py:23
  151.3 20.4 %copy-start.1 = (f32[512,512]{1,0:T(8,128)S(1)}, f32[512,512]{1,0:T(8,128)}, u32[]{:S(2)}) copy-start(f32[512,512]{1,0:T(8,128)} %all-reduce.2.cloned.1.call-done) | copy-start | bytes 3145732
  190.8 0.7 copy-start.2
Sparse Core Ops, SparseCore 0:
  20.1 131.1 all-reduce.1
where the time goes:
time: 217 us
  waiting for transfers between devices  131 us (60%)
  other arithmetic  34.9 us (16%)
  blocking collectives  26.7 us (12%)
  between operations  14.2 us (7%)
  matrix products  6.67 us (3%)
  local copies, waits for them, and re-layouts  2.77 us (1%)
    psum x1, waiting for transfers between devices, local(): lax.psum(fibre_gram(regrouped, regrouped), ('gx', 'yz')) / cell_count  131 us
    another operation x6, other arithmetic, orthonormal(): lower_factor = jnp.linalg.cholesky(small_gram)  18.9 us
    another operation x4, other arithmetic, orthonormal(): lax.linalg.triangular_solve(lower_factor, image_rows, left_side=True, low...  16 us
    all_to_all x1, blocking collectives, local(): lax.all_to_all(lax.all_to_all(core_local, 'gx', split_axis=0, concat_axis...  10.9 us
    all_to_all x1, blocking collectives, local(): lax.all_to_all(tensor, 'gx', split_axis=2, concat_axis=1, tiled=True)  9.21 us
    all_to_all x1, blocking collectives, local(): lax.all_to_all(core_local, 'gx', split_axis=0, concat_axis=1, tiled=True)  6.57 us
  transfers between devices with their start and end apart: 1, of which 1 were waited for; matrix products, arithmetic and copies ran while one was open for 0% of the time, Pallas kernels for 0%

commit v1 on v0

v1 whole, which is shorter than its diff:
```python
import functools

import jax
import jax.numpy as jnp
from jax import lax
from jax.experimental import pallas as pl
from jax.experimental.pallas import tpu as pltpu
from jax.sharding import PartitionSpec as P

HIGHEST = lax.Precision.HIGHEST
LANES = 128
SUBLANES = 8


def mm(a, b):
    return lax.dot_general(
        a, b, (((1,), (0,)), ((), ())), precision=HIGHEST, preferred_element_type=jnp.float32
    )


def mm_nt(a, b):
    return lax.dot_general(
        a, b, (((1,), (1,)), ((), ())), precision=HIGHEST, preferred_element_type=jnp.float32
    )


def inverse_cholesky(gram):
    rank = gram.shape[0]
    wide = -(-rank // LANES) * LANES
    row_id = lax.broadcasted_iota(jnp.int32, (rank, wide), 0)
    lane_id = lax.broadcasted_iota(jnp.int32, (rank, wide), 1)
    left = jnp.concatenate([gram, jnp.zeros((rank, wide - rank), jnp.float32)], axis=1) if wide > rank else gram
    right = jnp.where(row_id == lane_id, 1.0, 0.0).astype(jnp.float32)
    done_left, done_right = [], []
    for base in range(0, rank, SUBLANES):
        rows = rank - base
        local_row = lax.broadcasted_iota(jnp.int32, (rows, wide), 0)
        for step in range(SUBLANES):
            column = base + step
            pivot = left[step : step + 1, column : column + 1]
            inverse = 1.0 / jnp.broadcast_to(pivot, (1, wide))
            row_left = left[step : step + 1, :] * inverse
            row_right = right[step : step + 1, :] * inverse
            factor = jnp.broadcast_to(left[:, column : column + 1], (rows, wide))
            factor = jnp.where(local_row > step, factor, 0.0)
            left = left - factor * row_left
            right = right - factor * row_right
        done_left.append(left[:SUBLANES])
        done_right.append(right[:SUBLANES])
        left, right = left[SUBLANES:], right[SUBLANES:]
    upper = jnp.concatenate(done_left, axis=0)
    lower = jnp.concatenate(done_right, axis=0)
    pivots = jnp.sum(jnp.where(row_id == lane_id, upper, 0.0), axis=1, keepdims=True)
    return (lower / jnp.sqrt(pivots))[:, :rank]


def kernel(
    shape,
    x_ref,
    start_ref,
    core_ref,
    factor_ref,
    xg,
    stage,
    sums,
    parts,
    core_out,
    core_in,
    x_send,
    x_recv,
    send_sem,
    recv_sem,
):
    n_gx, n_yz, cell_count, rows = shape
    n = n_gx * n_yz
    my_x, my_yz = lax.axis_index("gx"), lax.axis_index("yz")
    me = my_x * n_yz + my_yz
    species, _, cells_z, width = x_ref.shape
    lines = xg.shape[2]
    rank, total = start_ref.shape
    per_column = rank // rows

    def place(flat):
        return {"gx": lax.div(flat, n_yz), "yz": lax.rem(flat, n_yz)}

    def ahead(k):
        return lax.rem(me + k, n)

    def behind(k):
        return lax.rem(me + n - k, n)

    barrier = pltpu.get_barrier_semaphore()

    @pl.loop(1, n)
    def _(k):
        pl.semaphore_signal(barrier, inc=1, device_id=place(ahead(k)), device_id_type=pl.DeviceIdType.MESH)

    xg[my_x] = x_ref[:, pl.ds(my_x * lines, lines)]
    pl.semaphore_wait(barrier, n - 1)

    def x_copy(k):
        peer = lax.rem(my_x + k, n_gx)
        return pltpu.make_async_remote_copy(
            src_ref=x_ref.at[:, pl.ds(peer * lines, lines)],
            dst_ref=xg.at[my_x],
            send_sem=x_send.at[k - 1],
            recv_sem=x_recv.at[k - 1],
            device_id={"gx": peer, "yz": my_yz},
            device_id_type=pl.DeviceIdType.MESH,
        )

    for k in range(1, n_gx):
        x_copy(k).start()
    for k in range(1, n_gx):
        x_copy(k).wait()

    def held(part):
        return xg[part].reshape(species * lines * cells_z, width)

    def image_of(basis):
        projected = None
        for part in range(n_gx):
            term = mm_nt(basis[:, part * width : (part + 1) * width], held(part))
            projected = term if projected is None else projected + term
        projected = projected * (1.0 / cell_count)
        return jnp.concatenate([mm(projected, held(part)) for part in range(n_gx)], axis=1)

    def scatter_copy(turn, k):
        peer = ahead(k)
        return pltpu.make_async_remote_copy(
            src_ref=stage.at[turn, peer],
            dst_ref=parts.at[turn, k - 1],
            send_sem=send_sem.at[k - 1],
            recv_sem=recv_sem.at[2 * turn, k - 1],
            device_id=place(peer),
            device_id_type=pl.DeviceIdType.MESH,
        )

    def gather_copy(turn, k):
        return pltpu.make_async_remote_copy(
            src_ref=sums.at[turn, me],
            dst_ref=sums.at[turn, me],
            send_sem=send_sem.at[k - 1],
            recv_sem=recv_sem.at[2 * turn + 1, k - 1],
            device_id=place(ahead(k)),
            device_id_type=pl.DeviceIdType.MESH,
        )

    def gather_arrival(turn, k):
        source = behind(k)
        return pltpu.make_async_remote_copy(
            src_ref=sums.at[turn, me],
            dst_ref=sums.at[turn, source],
            send_sem=send_sem.at[k - 1],
            recv_sem=recv_sem.at[2 * turn + 1, k - 1],
            device_id=place(ahead(k)),
            device_id_type=pl.DeviceIdType.MESH,
        )

    def start_scatter(turn, image):
        for owner in range(n):
            column, block = owner // per_column, owner % per_column
            stage[turn, owner] = image[block * rows : (block + 1) * rows, column * LANES : (column + 1) * LANES]

        @pl.loop(1, n)
        def _(k):
            scatter_copy(turn, k).start()

    def finish_sum(turn):
        @pl.loop(1, n)
        def _(k):
            scatter_copy(turn, k).wait()

        terms = [stage[turn, me]] + [parts[turn, k] for k in range(n - 1)]
        while len(terms) > 1:
            terms = [a + b for a, b in zip(terms[::2], terms[1::2])] + ([terms[-1]] if len(terms) % 2 else [])
        sums[turn, me] = terms[0]

        @pl.loop(1, n)
        def _(k):
            gather_copy(turn, k).start()

        @pl.loop(1, n)
        def _(k):
            gather_arrival(turn, k).wait()

        columns = []
        for column in range(total // LANES):
            blocks = [sums[turn, column * per_column + block] for block in range(per_column)]
            columns.append(jnp.concatenate(blocks, axis=0))
        return jnp.concatenate(columns, axis=1)

    start_scatter(0, image_of(start_ref[...]))
    image = finish_sum(0)
    start_scatter(1, image_of(image))
    inverse = inverse_cholesky(mm_nt(image, image))
    image = mm(inverse, finish_sum(1))
    basis = mm(inverse_cholesky(mm_nt(image, image)), image)
    factor_ref[...] = basis

    truncated = None
    for part in range(n_gx):
        term = mm_nt(held(part), basis[:, part * width : (part + 1) * width])
        truncated = term if truncated is None else truncated + term
    share = cells_z // n
    for s in range(species):
        for line in range(lines):
            at = (s * lines + line) * cells_z
            core_out[:, line, s * rank : (s + 1) * rank] = truncated[at : at + cells_z]

    mine = my_yz * n_gx + my_x

    def core_copy(k):
        peer = ahead(k)
        return pltpu.make_async_remote_copy(
            src_ref=core_out.at[pl.ds(peer * share, share)],
            dst_ref=core_in.at[mine],
            send_sem=send_sem.at[k - 1],
            recv_sem=recv_sem.at[4, k - 1],
            device_id=place(peer),
            device_id_type=pl.DeviceIdType.MESH,
        )

    def core_arrival(k):
        source = behind(k)
        place_of = lax.rem(source, n_yz) * n_gx + lax.div(source, n_yz)
        return pltpu.make_async_remote_copy(
            src_ref=core_out.at[pl.ds(ahead(k) * share, share)],
            dst_ref=core_in.at[place_of],
            send_sem=send_sem.at[k - 1],
            recv_sem=recv_sem.at[4, k - 1],
            device_id=place(ahead(k)),
            device_id_type=pl.DeviceIdType.MESH,
        )

    @pl.loop(1, n)
    def _(k):
        core_copy(k).start()

    core_in[mine] = core_out[pl.ds(me * share, share)]

    @pl.loop(1, n)
    def _(k):
        core_arrival(k).wait()

    core_ref[...] = core_in[...]


def kernel_program(tensor, start_basis, n_gx, n_yz, rows):
    n = n_gx * n_yz
    species, width, lines_held, cells_z = tensor.shape
    rank, total = start_basis.shape
    lines = lines_held // n_gx
    cell_count = species * lines_held * n_yz * cells_z
    share = cells_z // n
    out = species * rank
    core, factor = pl.pallas_call(
        functools.partial(kernel, (n_gx, n_yz, cell_count, rows)),
        out_shape=(
            jax.ShapeDtypeStruct((n, share, lines, out), jnp.float32),
            jax.ShapeDtypeStruct((rank, total), jnp.float32),
        ),
        in_specs=[pl.BlockSpec(memory_space=pltpu.VMEM)] * 2,
        out_specs=(pl.BlockSpec(memory_space=pltpu.VMEM),) * 2,
        scratch_shapes=[
            pltpu.VMEM((n_gx, species, lines, cells_z, width), jnp.float32),
            pltpu.VMEM((2, n, rows, LANES), jnp.float32),
            pltpu.VMEM((2, n, rows, LANES), jnp.float32),
            pltpu.VMEM((2, n - 1, rows, LANES), jnp.float32),
            pltpu.VMEM((cells_z, lines, out), jnp.float32),
            pltpu.VMEM((n, share, lines, out), jnp.float32),
            pltpu.SemaphoreType.DMA((n_gx - 1,)),
            pltpu.SemaphoreType.DMA((n_gx - 1,)),
            pltpu.SemaphoreType.DMA((n - 1,)),
            pltpu.SemaphoreType.DMA((5, n - 1)),
        ],
        compiler_params=pltpu.CompilerParams(collective_id=0, has_side_effects=True),
    )(tensor.transpose(0, 2, 3, 1), start_basis)
    core = core.transpose(1, 0, 2, 3).reshape(share, n * lines, out)
    return core, factor


def orthonormal(image_rows):
    small_gram = jnp.dot(image_rows, image_rows.T, precision=HIGHEST)
    lower_factor = jnp.linalg.cholesky(small_gram)
    return lax.linalg.triangular_solve(lower_factor, image_rows, left_side=True, lower=True)


def collective_program(tensor, start_basis):
    regrouped = lax.all_to_all(tensor, "gx", split_axis=2, concat_axis=1, tiled=True)
    species, _, lines, cells_z = regrouped.shape
    cell_count = species * lines * lax.axis_size("gx") * lax.axis_size("yz") * cells_z
    gram_matrix = lax.dot_general(
        regrouped, regrouped, (((0, 2, 3), (0, 2, 3)), ((), ())), precision=HIGHEST
    )
    gram_matrix = lax.psum(gram_matrix, ("gx", "yz")) / cell_count
    basis = start_basis
    for _ in range(2):
        basis = orthonormal(jnp.dot(basis, gram_matrix, precision=HIGHEST))
    core_local = jnp.einsum("kx,sxyz->zysk", basis, regrouped, precision=HIGHEST)
    core_local = core_local.reshape(cells_z, lines, species * basis.shape[0])
    core_tensor = lax.all_to_all(
        lax.all_to_all(core_local, "gx", split_axis=0, concat_axis=1, tiled=True),
        "yz",
        split_axis=0,
        concat_axis=1,
        tiled=True,
    )
    return core_tensor, basis


def solution(mesh):
    n_gx, n_yz = mesh.shape["gx"], mesh.shape["yz"]
    n = n_gx * n_yz

    def local(tensor, start_basis):
        rank, total = start_basis.shape
        rows, left_over = divmod(rank * (total // LANES), n)
        whole_rows = left_over == 0 and total % LANES == 0 and rank % max(rows, 1) == 0 and rank % SUBLANES == 0
        if whole_rows and tensor.shape[1] % LANES == 0:
            return kernel_program(tensor, start_basis, n_gx, n_yz, rows)
        return collective_program(tensor, start_basis)

    return jax.shard_map(
        local,
        mesh=mesh,
        in_specs=(P(None, "gx", "yz", None), P()),
        out_specs=(P(("gx", "yz"), None, None), P()),
        check_vma=False,
    )
```

time: 217 us -> 64.1 us (0.30)
  waiting for transfers between devices: 131 us -> 0 us
  Pallas kernels: 0 us -> 60.2 us
  other arithmetic: 34.9 us -> 0 us
  blocking collectives: 26.7 us -> 0 us
  between operations: 14.2 us -> 0.64 us
  matrix products: 6.67 us -> 0 us
    psum x1 -> x0, waiting for transfers between devices: 131 us -> none  [local(): lax.psum(fibre_gram(regrouped, regrouped), ('gx', 'yz')) / cell_count]
    pallas_call x0 -> x1, Pallas kernels: none -> 60.2 us  [kernel_program(): pl.pallas_call(functools.partial(kernel, (n_gx, n_yz, cell_count, rows)),...]
    another operation x10 -> x0, other arithmetic: 34.9 us -> none  [the longest x6 18.9 us: orthonormal(): lower_factor = jnp.linalg.cholesky(small_gram)]
    all_to_all x3 -> x0, blocking collectives: 26.7 us -> none  [the longest x1 10.9 us: local(): lax.all_to_all(lax.all_to_all(core_local, 'gx', split_axis=0, concat_axis...]
    dot_general x5 -> x0, matrix products: 5.55 us -> none  [the longest x2 2.85 us: local(): jnp.dot(basis, gram_matrix, precision=lax.Precision.HIGHEST)]
  transfers between devices with their start and end apart: 1 -> 0, of which waited for: 1 -> 0; matrix products, arithmetic and copies ran while one was open for 0% -> 0% of each run, Pallas kernels for 0% -> 0%
where the time goes in v1:
time: 64.1 us; the launch traced here: 63.9 us
  Pallas kernels  60.2 us (94%)
  local copies, waits for them, and re-layouts  3.04 us (5%)
    pallas_call x1, Pallas kernels, kernel_program(): pl.pallas_call(functools.partial(kernel, (n_gx, n_yz, cell_count, rows)),...  60.2 us
    unnamed x2, local copies, waits for them, and re-layouts  3.04 us

profile of v1, /device:TPU:0, one launch (start us, length us, event | category | flops | bytes accessed | tf_op | source)
XLA Modules:
  0.0 63.9 jit_solution(14941650516981599168)
XLA Ops:
  0.6 60.2 %shard_map.41 = (f32[32,1,1,384]{3,2,1,0:T(1,128)}, f32[96,512]{1,0:T(8,128)}) custom-call(f32[4,2,32,256]{3,2,1,0:T(8,128)} %bitcast.2, f32[96,512]{1,0:T(8,128)} %start_ref.1), custom_call_target="tpu_custom_call" | custom-call | tf_op jit(solution)/shard_map/pallas_call | solution.py:257
  60.8 1.4 %copy.4 = f32[1,32,384]{2,1,0:T(8,128)} copy(f32[1,32,384]{2,0,1:T(1,128)} %bitcast.3) | data formatting | bytes 98304
  62.2 1.6 %copy.6 = f32[96,512]{1,0:T(8,128)} copy(f32[96,512]{1,0:T(8,128)} %get-tuple-element.11) | data formatting | bytes 393216

commit v2 on v1

--- a/solution.py
+++ b/solution.py
@@ -24,34 +24,35 @@
     )
 
 
-def inverse_cholesky(gram):
+def inverse_cholesky(gram, panel=SUBLANES):
     rank = gram.shape[0]
     wide = -(-rank // LANES) * LANES
     row_id = lax.broadcasted_iota(jnp.int32, (rank, wide), 0)
     lane_id = lax.broadcasted_iota(jnp.int32, (rank, wide), 1)
     left = jnp.concatenate([gram, jnp.zeros((rank, wide - rank), jnp.float32)], axis=1) if wide > rank else gram
     right = jnp.where(row_id == lane_id, 1.0, 0.0).astype(jnp.float32)
-    done_left, done_right = [], []
+    done_right, done_pivots = [], []
     for base in range(0, rank, SUBLANES):
         rows = rank - base
         local_row = lax.broadcasted_iota(jnp.int32, (rows, wide), 0)
-        for step in range(SUBLANES):
-            column = base + step
-            pivot = left[step : step + 1, column : column + 1]
-            inverse = 1.0 / jnp.broadcast_to(pivot, (1, wide))
-            row_left = left[step : step + 1, :] * inverse
-            row_right = right[step : step + 1, :] * inverse
-            factor = jnp.broadcast_to(left[:, column : column + 1], (rows, wide))
-            factor = jnp.where(local_row > step, factor, 0.0)
-            left = left - factor * row_left
-            right = right - factor * row_right
-        done_left.append(left[:SUBLANES])
-        done_right.append(right[:SUBLANES])
+        pivots = jnp.zeros((SUBLANES, wide), jnp.float32)
+        for first in range(0, SUBLANES, panel):
+            spread = [
+                jnp.broadcast_to(left[:, base + step : base + step + 1], (rows, wide))
+                for step in range(first, first + panel)
+            ]
+            for step in range(first, first + panel):
+                column = spread[step - first]
+                pivot = column[step : step + 1]
+                pivots = jnp.where(local_row[:SUBLANES] == step, jnp.broadcast_to(pivot, (SUBLANES, wide)), pivots)
+                factor = jnp.where(local_row > step, column * (1.0 / pivot), 0.0)
+                for other in range(step + 1, first + panel):
+                    spread[other - first] = spread[other - first] - factor * spread[other - first][step : step + 1]
+                left = left - factor * left[step : step + 1]
+                right = right - factor * right[step : step + 1]
+        done_right.append(right[:SUBLANES] / jnp.sqrt(pivots))
         left, right = left[SUBLANES:], right[SUBLANES:]
-    upper = jnp.concatenate(done_left, axis=0)
-    lower = jnp.concatenate(done_right, axis=0)
-    pivots = jnp.sum(jnp.where(row_id == lane_id, upper, 0.0), axis=1, keepdims=True)
-    return (lower / jnp.sqrt(pivots))[:, :rank]
+    return jnp.concatenate(done_right, axis=0)[:, :rank]
 
 
 def kernel(
@@ -79,21 +80,19 @@
     lines = xg.shape[2]
     rank, total = start_ref.shape
     per_column = rank // rows
+    order = range(n - 1, 0, -1)
+    flips = [1 - 2 * lax.rem(lax.div(me, 1 << bit), 2) for bit in range(n.bit_length() - 1)]
 
     def place(flat):
         return {"gx": lax.div(flat, n_yz), "yz": lax.rem(flat, n_yz)}
 
-    def ahead(k):
-        return lax.rem(me + k, n)
-
-    def behind(k):
-        return lax.rem(me + n - k, n)
+    def partner(k):
+        return me + sum((1 << bit) * flip for bit, flip in enumerate(flips) if k >> bit & 1)
 
     barrier = pltpu.get_barrier_semaphore()
 
-    @pl.loop(1, n)
-    def _(k):
-        pl.semaphore_signal(barrier, inc=1, device_id=place(ahead(k)), device_id_type=pl.DeviceIdType.MESH)
+    for k in order:
+        pl.semaphore_signal(barrier, inc=1, device_id=place(partner(k)), device_id_type=pl.DeviceIdType.MESH)
 
     xg[my_x] = x_ref[:, pl.ds(my_x * lines, lines)]
     pl.semaphore_wait(barrier, n - 1)
@@ -126,11 +125,11 @@
         return jnp.concatenate([mm(projected, held(part)) for part in range(n_gx)], axis=1)
 
     def scatter_copy(turn, k):
-        peer = ahead(k)
+        peer = partner(k)
         return pltpu.make_async_remote_copy(
             src_ref=stage.at[turn, peer],
             dst_ref=parts.at[turn, k - 1],
-            send_sem=send_sem.at[k - 1],
+            send_sem=send_sem.at[2 * turn, k - 1],
             recv_sem=recv_sem.at[2 * turn, k - 1],
             device_id=place(peer),
             device_id_type=pl.DeviceIdType.MESH,
@@ -140,20 +139,20 @@
         return pltpu.make_async_remote_copy(
             src_ref=sums.at[turn, me],
             dst_ref=sums.at[turn, me],
-            send_sem=send_sem.at[k - 1],
+            send_sem=send_sem.at[2 * turn + 1, k - 1],
             recv_sem=recv_sem.at[2 * turn + 1, k - 1],
-            device_id=place(ahead(k)),
+            device_id=place(partner(k)),
             device_id_type=pl.DeviceIdType.MESH,
         )
 
     def gather_arrival(turn, k):
-        source = behind(k)
+        source = partner(k)
         return pltpu.make_async_remote_copy(
             src_ref=sums.at[turn, me],
             dst_ref=sums.at[turn, source],
-            send_sem=send_sem.at[k - 1],
+            send_sem=send_sem.at[2 * turn + 1, k - 1],
             recv_sem=recv_sem.at[2 * turn + 1, k - 1],
-            device_id=place(ahead(k)),
+            device_id=place(partner(k)),
             device_id_type=pl.DeviceIdType.MESH,
         )
 
@@ -161,40 +160,35 @@
         for owner in range(n):
             column, block = owner // per_column, owner % per_column
             stage[turn, owner] = image[block * rows : (block + 1) * rows, column * LANES : (column + 1) * LANES]
-
-        @pl.loop(1, n)
-        def _(k):
+        for k in order:
             scatter_copy(turn, k).start()
 
-    def finish_sum(turn):
-        @pl.loop(1, n)
-        def _(k):
-            scatter_copy(turn, k).wait()
-
+    def start_gather(turn):
+        for k in order:
+            scatter_copy(turn, k).wait_recv()
         terms = [stage[turn, me]] + [parts[turn, k] for k in range(n - 1)]
         while len(terms) > 1:
             terms = [a + b for a, b in zip(terms[::2], terms[1::2])] + ([terms[-1]] if len(terms) % 2 else [])
         sums[turn, me] = terms[0]
-
-        @pl.loop(1, n)
-        def _(k):
+        for k in order:
             gather_copy(turn, k).start()
-
-        @pl.loop(1, n)
-        def _(k):
-            gather_arrival(turn, k).wait()
-
-        columns = []
-        for column in range(total // LANES):
-            blocks = [sums[turn, column * per_column + block] for block in range(per_column)]
-            columns.append(jnp.concatenate(blocks, axis=0))
+        for k in order:
+            scatter_copy(turn, k).wait_send()
+
+    def gathered(turn):
+        for k in order:
+            gather_arrival(turn, k).wait_recv()
+        blocks = [sums[turn, owner] for owner in range(n)]
+        columns = [jnp.concatenate(blocks[at : at + per_column], axis=0) for at in range(0, n, per_column)]
         return jnp.concatenate(columns, axis=1)
 
     start_scatter(0, image_of(start_ref[...]))
-    image = finish_sum(0)
+    start_gather(0)
+    image = gathered(0)
     start_scatter(1, image_of(image))
+    start_gather(1)
     inverse = inverse_cholesky(mm_nt(image, image))
-    image = mm(inverse, finish_sum(1))
+    image = mm(inverse, gathered(1))
     basis = mm(inverse_cholesky(mm_nt(image, image)), image)
     factor_ref[...] = basis
 
@@ -211,36 +205,36 @@
     mine = my_yz * n_gx + my_x
 
     def core_copy(k):
-        peer = ahead(k)
+        peer = partner(k)
         return pltpu.make_async_remote_copy(
             src_ref=core_out.at[pl.ds(peer * share, share)],
             dst_ref=core_in.at[mine],
-            send_sem=send_sem.at[k - 1],
+            send_sem=send_sem.at[4, k - 1],
             recv_sem=recv_sem.at[4, k - 1],
             device_id=place(peer),
             device_id_type=pl.DeviceIdType.MESH,
         )
 
     def core_arrival(k):
-        source = behind(k)
+        source = partner(k)
         place_of = lax.rem(source, n_yz) * n_gx + lax.div(source, n_yz)
         return pltpu.make_async_remote_copy(
-            src_ref=core_out.at[pl.ds(ahead(k) * share, share)],
+            src_ref=core_out.at[pl.ds(partner(k) * share, share)],
             dst_ref=core_in.at[place_of],
-            send_sem=send_sem.at[k - 1],
+            send_sem=send_sem.at[4, k - 1],
             recv_sem=recv_sem.at[4, k - 1],
-            device_id=place(ahead(k)),
-            device_id_type=pl.DeviceIdType.MESH,
-        )
-
-    @pl.loop(1, n)
-    def _(k):
+            device_id=place(partner(k)),
+            device_id_type=pl.DeviceIdType.MESH,
+        )
+
+    for k in order:
         core_copy(k).start()
 
     core_in[mine] = core_out[pl.ds(me * share, share)]
 
-    @pl.loop(1, n)
-    def _(k):
+    for k in order:
+        for turn in range(2):
+            gather_copy(turn, k).wait_send()
         core_arrival(k).wait()
 
     core_ref[...] = core_in[...]
@@ -257,8 +251,8 @@
     core, factor = pl.pallas_call(
         functools.partial(kernel, (n_gx, n_yz, cell_count, rows)),
         out_shape=(
-            jax.ShapeDtypeStruct((n, share, lines, out), jnp.float32),
-            jax.ShapeDtypeStruct((rank, total), jnp.float32),
+            pltpu.VMEM((n, share, lines, out), jnp.float32),
+            pltpu.VMEM((rank, total), jnp.float32),
         ),
         in_specs=[pl.BlockSpec(memory_space=pltpu.VMEM)] * 2,
         out_specs=(pl.BlockSpec(memory_space=pltpu.VMEM),) * 2,
@@ -271,7 +265,7 @@
             pltpu.VMEM((n, share, lines, out), jnp.float32),
             pltpu.SemaphoreType.DMA((n_gx - 1,)),
             pltpu.SemaphoreType.DMA((n_gx - 1,)),
-            pltpu.SemaphoreType.DMA((n - 1,)),
+            pltpu.SemaphoreType.DMA((5, n - 1)),
             pltpu.SemaphoreType.DMA((5, n - 1)),
         ],
         compiler_params=pltpu.CompilerParams(collective_id=0, has_side_effects=True),
@@ -316,7 +310,8 @@
     def local(tensor, start_basis):
         rank, total = start_basis.shape
         rows, left_over = divmod(rank * (total // LANES), n)
-        whole_rows = left_over == 0 and total % LANES == 0 and rank % max(rows, 1) == 0 and rank % SUBLANES == 0
+        whole_rows = left_over == 0 and total % LANES == 0 and n & (n - 1) == 0
+        whole_rows = whole_rows and rank % max(rows, 1) == 0 and rank % SUBLANES == 0
         if whole_rows and tensor.shape[1] % LANES == 0:
             return kernel_program(tensor, start_basis, n_gx, n_yz, rows)
         return collective_program(tensor, start_basis)

time: 64.1 us -> 51.9 us (0.81)
  Pallas kernels: 60.2 us -> 49.8 us
  local copies, waits for them, and re-layouts: 3.04 us -> 1.3 us
    pallas_call x1, Pallas kernels: 60.2 us -> 49.8 us  [kernel_program(): pl.pallas_call(functools.partial(kernel, (n_gx, n_yz, cell_count, rows)),...]
    unnamed x2, local copies, waits for them, and re-layouts: 3.04 us -> 1.3 us
where the time goes in v2:
time: 51.9 us; the launch traced here: 51.7 us
  Pallas kernels  49.8 us (96%)
  local copies, waits for them, and re-layouts  1.3 us (3%)
  between operations  0.64 us (1%)
    pallas_call x1, Pallas kernels, kernel_program(): pl.pallas_call(functools.partial(kernel, (n_gx, n_yz, cell_count, rows)),...  49.8 us
    unnamed x2, local copies, waits for them, and re-layouts  1.3 us

profile of v2, /device:TPU:0, one launch (start us, length us, event | category | flops | bytes accessed | tf_op | source)
XLA Modules:
  0.0 51.7 jit_solution(6118845357310764207)
XLA Ops:
  0.6 49.8 %shard_map.41 = (f32[32,1,1,384]{3,2,1,0:T(1,128)S(1)}, f32[96,512]{1,0:T(8,128)S(1)}) custom-call(f32[4,2,32,256]{3,2,1,0:T(8,128)} %bitcast.3, f32[96,512]{1,0:T(8,128)} %start_ref.1), custom_call_target="tpu_custom_call" | custom-call | tf_op jit(solution)/shard_map/pallas_call | solution.py:251
  50.4 0.6 %copy.4 = f32[1,32,384]{2,1,0:T(8,128)} copy(f32[1,32,384]{2,0,1:T(1,128)S(1)} %bitcast.2) | data formatting | bytes 98304
  51.0 0.7 %copy.6 = f32[96,512]{1,0:T(8,128)} copy(f32[96,512]{1,0:T(8,128)S(1)} %get-tuple-element.9) | data formatting | bytes 393216

commit v3 on v2

--- a/solution.py
+++ b/solution.py
@@ -64,6 +64,7 @@
     xg,
     stage,
     sums,
+    pairs,
     parts,
     core_out,
     core_in,
@@ -81,6 +82,8 @@
     rank, total = start_ref.shape
     per_column = rank // rows
     order = range(n - 1, 0, -1)
+    odds = range(n - 1, 0, -2)
+    direct = [*range(n - 2, 0, -2), 1]
     flips = [1 - 2 * lax.rem(lax.div(me, 1 << bit), 2) for bit in range(n.bit_length() - 1)]
 
     def place(flat):
@@ -125,13 +128,13 @@
         return jnp.concatenate([mm(projected, held(part)) for part in range(n_gx)], axis=1)
 
     def scatter_copy(turn, k):
-        peer = partner(k)
-        return pltpu.make_async_remote_copy(
-            src_ref=stage.at[turn, peer],
-            dst_ref=parts.at[turn, k - 1],
+        odd = k % 2
+        return pltpu.make_async_remote_copy(
+            src_ref=stage.at[turn, partner(k)],
+            dst_ref=pairs.at[turn, k // 2] if odd else parts.at[turn, k // 2 - 1],
             send_sem=send_sem.at[2 * turn, k - 1],
             recv_sem=recv_sem.at[2 * turn, k - 1],
-            device_id=place(peer),
+            device_id=place(partner(1) if odd else partner(k)),
             device_id_type=pl.DeviceIdType.MESH,
         )
 
@@ -145,6 +148,17 @@
             device_id_type=pl.DeviceIdType.MESH,
         )
 
+    def relay_copy(turn, k):
+        source = partner(k)
+        return pltpu.make_async_remote_copy(
+            src_ref=sums.at[turn, source],
+            dst_ref=sums.at[turn, source],
+            send_sem=send_sem.at[2 * turn + 1, k],
+            recv_sem=recv_sem.at[2 * turn + 1, k],
+            device_id=place(partner(1)),
+            device_id_type=pl.DeviceIdType.MESH,
+        )
+
     def gather_arrival(turn, k):
         source = partner(k)
         return pltpu.make_async_remote_copy(
@@ -160,24 +174,34 @@
         for owner in range(n):
             column, block = owner // per_column, owner % per_column
             stage[turn, owner] = image[block * rows : (block + 1) * rows, column * LANES : (column + 1) * LANES]
-        for k in order:
+        for k in odds:
             scatter_copy(turn, k).start()
+        for k in odds:
+            scatter_copy(turn, k).wait_recv()
+            stage[turn, partner(k - 1)] = stage[turn, partner(k - 1)] + pairs[turn, k // 2]
+            if k > 1:
+                scatter_copy(turn, k - 1).start()
 
     def start_gather(turn):
-        for k in order:
-            scatter_copy(turn, k).wait_recv()
-        terms = [stage[turn, me]] + [parts[turn, k] for k in range(n - 1)]
+        for k in odds[:-1]:
+            scatter_copy(turn, k - 1).wait_recv()
+        terms = [stage[turn, me]] + [parts[turn, k] for k in range(n // 2 - 1)]
         while len(terms) > 1:
             terms = [a + b for a, b in zip(terms[::2], terms[1::2])] + ([terms[-1]] if len(terms) % 2 else [])
         sums[turn, me] = terms[0]
-        for k in order:
+        for k in direct:
             gather_copy(turn, k).start()
         for k in order:
             scatter_copy(turn, k).wait_send()
 
     def gathered(turn):
-        for k in order:
+        for k in direct:
             gather_arrival(turn, k).wait_recv()
+            if k > 1:
+                relay_copy(turn, k).start()
+        for k in direct:
+            if k > 1:
+                relay_copy(turn, k).wait_recv()
         blocks = [sums[turn, owner] for owner in range(n)]
         columns = [jnp.concatenate(blocks[at : at + per_column], axis=0) for at in range(0, n, per_column)]
         return jnp.concatenate(columns, axis=1)
@@ -234,7 +258,10 @@
 
     for k in order:
         for turn in range(2):
-            gather_copy(turn, k).wait_send()
+            if k in direct:
+                gather_copy(turn, k).wait_send()
+            else:
+                relay_copy(turn, k - 1).wait_send()
         core_arrival(k).wait()
 
     core_ref[...] = core_in[...]
@@ -260,7 +287,8 @@
             pltpu.VMEM((n_gx, species, lines, cells_z, width), jnp.float32),
             pltpu.VMEM((2, n, rows, LANES), jnp.float32),
             pltpu.VMEM((2, n, rows, LANES), jnp.float32),
-            pltpu.VMEM((2, n - 1, rows, LANES), jnp.float32),
+            pltpu.VMEM((2, n // 2, rows, LANES), jnp.float32),
+            pltpu.VMEM((2, n // 2 - 1, rows, LANES), jnp.float32),
             pltpu.VMEM((cells_z, lines, out), jnp.float32),
             pltpu.VMEM((n, share, lines, out), jnp.float32),
             pltpu.SemaphoreType.DMA((n_gx - 1,)),

time: 51.9 us -> 48.7 us (0.938)
  Pallas kernels: 49.8 us -> 46.6 us
    pallas_call x1, Pallas kernels: 49.8 us -> 46.6 us  [kernel_program(): pl.pallas_call(functools.partial(kernel, (n_gx, n_yz, cell_count, rows)),...]
where the time goes in v3:
time: 48.7 us; the launch traced here: 48.5 us
  Pallas kernels  46.6 us (96%)
  local copies, waits for them, and re-layouts  1.3 us (3%)
  between operations  0.64 us (1%)
    pallas_call x1, Pallas kernels, kernel_program(): pl.pallas_call(functools.partial(kernel, (n_gx, n_yz, cell_count, rows)),...  46.6 us
    unnamed x2, local copies, waits for them, and re-layouts  1.3 us

profile of v3, /device:TPU:0, one launch (start us, length us, event | category | flops | bytes accessed | tf_op | source)
XLA Modules:
  0.0 48.5 jit_solution(3703095252934936199)
XLA Ops:
  0.6 46.6 %shard_map.41 = (f32[32,1,1,384]{3,2,1,0:T(1,128)S(1)}, f32[96,512]{1,0:T(8,128)S(1)}) custom-call(f32[4,2,32,256]{3,2,1,0:T(8,128)} %bitcast.3, f32[96,512]{1,0:T(8,128)} %start_ref.1), custom_call_target="tpu_custom_call" | custom-call | tf_op jit(solution)/shard_map/pallas_call | solution.py:278
  47.2 0.6 %copy.4 = f32[1,32,384]{2,1,0:T(8,128)} copy(f32[1,32,384]{2,0,1:T(1,128)S(1)} %bitcast.2) | data formatting | bytes 98304
  47.9 0.7 %copy.6 = f32[96,512]{1,0:T(8,128)} copy(f32[96,512]{1,0:T(8,128)S(1)} %get-tuple-element.9) | data formatting | bytes 393216
